TPU v7x, 128 devices: a whole 4x4x4 slice. The times are simulated.
128 devices in a mesh: section: 16 (over y, z), dom: 8 (over x, core).
Axes of the slice: x: 4, y: 4, z: 4, core: 2. Of those that a mesh axis runs over, the one named last changes fastest.
Arguments:
- features: bfloat16 [12, 2048, 256], P(None, 'dom'), may hold values from -6 to 6
- cotangent: bfloat16 [12, 2048, 256], P(None, 'dom'), may hold values from -3 to 3
- weights: bfloat16 [16, 256, 256], P('section'), may hold values from -0.375 to 0.375
- tiles: bfloat16 [16, 6, 128, 128], P('dom'), may hold values from 0.0005 to 1
- sources: int32 [16, 6], P('dom'), may hold values from 0 to 15, as said below
- counts: int32 [16], P('dom'), may hold values from 1 to 6
Outputs:
- weight_grads: float32 [16, 256, 256], P('section')
Inputs may be any that keep to these rules, and one draw needn't show every extreme that they name: `sources`: entry 0 of each block's list is the block itself; every entry, used or not, names a block that lies on the same index of dom or is the block just before or just after that index's blocks.
All inputs are finite; a program needn't handle non-finite values.
Results may differ from a plain program's by a relative error of at most 0.02.
Values may be sent and summed in bfloat16 or wider, within the bound.
A program may use at most 64 MiB of HBM per device.

v0:
```python
import math

import jax
import jax.numpy as jnp
from jax import lax
from jax.sharding import PartitionSpec as P

epsilon = 1e-06


def extended(cells, sides, width):
    for axis, dim in sides:
        count = lax.axis_size(axis)
        ends = count - 1
        head = lax.slice_in_dim(cells, 0, width, axis=dim)
        tail = lax.slice_in_dim(cells, cells.shape[dim] - width, cells.shape[dim], axis=dim)
        cells = jnp.concatenate(
            [
                lax.ppermute(tail, axis, [(i, (i + 1) % count) for i in range(ends)]),
                cells,
                lax.ppermute(head, axis, [((i + 1) % count, i) for i in range(ends)]),
            ],
            axis=dim,
        )
    return cells


def passed_along(array, axis, by):
    size = lax.axis_size(axis)
    pairs = [(i, i + by) for i in range(size) if 0 <= i + by < size]
    return lax.ppermute(array, axis, pairs)


def block_setup(tiles, sources, counts):
    width = sources.shape[1]
    nblk = sources.shape[0]
    used = (jnp.arange(width)[None, :] < counts[:, None]).astype(tiles.dtype)
    masked = tiles * used[:, :, None, None]
    degree = jnp.sum(masked, axis=(1, 3), dtype=jnp.float32)
    first = lax.axis_index("dom") * nblk - 1
    local_src = sources - first
    onehot = (local_src[:, :, None] == jnp.arange(nblk + 2)[None, None, :]).astype(jnp.float32)
    return (masked, degree, local_src, onehot)


def widen(hidden, bsize):
    return extended(hidden, (("dom", 0),), bsize)


def aggregate(padded, masked, degree, local_src):
    nblk, bsize = degree.shape
    blocks = padded.reshape(nblk + 2, bsize, padded.shape[1])
    picked = jnp.take(blocks, local_src, axis=0)
    summed = jnp.einsum("bkij,bkjh->bih", masked, picked, preferred_element_type=jnp.float32)
    return (summed / degree[:, :, None]).reshape(nblk * bsize, padded.shape[1])


def normalize(agg):
    scale = lax.rsqrt(jnp.mean(agg * agg, axis=-1, keepdims=True) + epsilon)
    return ((agg * scale).astype(jnp.bfloat16), scale)


def project(agg, weight):
    nrm, scale = normalize(agg)
    return jnp.dot(nrm, weight, preferred_element_type=jnp.float32)


def keep_state(agg, z_val):
    return (agg, z_val)


def restore(saved):
    return (saved[0], saved[1])


def forward_layer(hidden, weight, setup):
    bsize = setup[1].shape[1]
    padded = widen(hidden, bsize)
    agg = aggregate(padded, setup[0], setup[1], setup[2])
    z_val = project(agg, weight)
    output = (hidden.astype(jnp.float32) + jax.nn.silu(z_val)).astype(jnp.bfloat16)
    return (output, keep_state(agg, z_val))


def backward_layer(grad_bf, agg, z_val, weight, setup):
    masked, degree, local_src, onehot = setup
    nblk, bsize = degree.shape
    grad = grad_bf.astype(jnp.float32)
    nrm, scale = normalize(agg)
    sig = jax.nn.sigmoid(z_val)
    dz_val = (grad * sig * (1.0 + z_val * (1.0 - sig))).astype(jnp.bfloat16)
    dweight = jnp.einsum("nh,nk->hk", nrm, dz_val, preferred_element_type=jnp.float32)
    dnrm = jnp.dot(dz_val, weight.T, preferred_element_type=jnp.float32)
    dagg = scale * (dnrm - agg * scale * scale * jnp.mean(dnrm * agg, axis=-1, keepdims=True))
    dsum = (dagg.reshape(nblk, bsize, -1) / degree[:, :, None]).astype(jnp.bfloat16)
    dpicked = jnp.einsum("bkij,bih->bkjh", masked, dsum, preferred_element_type=jnp.float32)
    dpad = jnp.einsum("bkc,bkjh->cjh", onehot, dpicked, precision=lax.Precision.HIGHEST)
    rims = jnp.concatenate([dpad[0], dpad[nblk + 1]], axis=0)
    outer = extended(rims.astype(jnp.bfloat16), (("dom", 0),), bsize).astype(rims.dtype)
    inner = dpad[1 : nblk + 1]
    inner = inner.at[0].add(outer[:bsize]).at[nblk - 1].add(outer[3 * bsize :])
    result = (grad + inner.reshape(nblk * bsize, -1)).astype(jnp.bfloat16)
    return (result, dweight)


def pick_slot(store, slot):
    return jax.tree.map(lambda item: lax.dynamic_index_in_dim(item, slot, 0, False), store)


def put_slot(store, value, slot, active):

    def update(item, fresh):
        older = lax.dynamic_index_in_dim(item, slot, 0, False)
        return lax.dynamic_update_index_in_dim(item, jnp.where(active, fresh, older), slot, 0)

    return jax.tree.map(update, store, value)


def local(features, cotangent, weights, tiles, sources, counts):
    setup = block_setup(tiles, sources, counts)
    count = features.shape[0]
    rows = features.shape[1]
    feats = features.shape[2]
    sections = lax.axis_size("section")
    section = lax.axis_index("section")
    weight = weights[0]
    steps = count + sections - 1
    store = (
        jnp.zeros((count, rows, feats), jnp.float32),
        jnp.zeros((count, rows, feats), jnp.float32),
    )

    def forward_step(step, carry):
        incoming, saved_all = carry
        slot_raw = step - section
        active = (slot_raw >= 0) & (slot_raw < count)
        slot = jnp.clip(slot_raw, 0, count - 1)
        hidden = jnp.where(
            section == 0, lax.dynamic_index_in_dim(features, slot, 0, False), incoming
        )
        output, saved = forward_layer(hidden, weight, setup)
        saved_all = put_slot(saved_all, saved, slot, active)
        outgoing = passed_along(output, "section", 1)
        return (outgoing, saved_all)

    start = jnp.zeros((rows, feats), jnp.bfloat16)
    last_in, store = lax.fori_loop(0, steps, forward_step, (start, store))

    def backward_step(step, carry):
        incoming, total = carry
        slot_raw = step - (sections - 1 - section)
        active = (slot_raw >= 0) & (slot_raw < count)
        slot = jnp.clip(slot_raw, 0, count - 1)
        agg, z_val = restore(pick_slot(store, slot))
        grad_in = jnp.where(
            section == sections - 1, lax.dynamic_index_in_dim(cotangent, slot, 0, False), incoming
        )
        result, dweight = backward_layer(grad_in, agg, z_val, weight, setup)
        total = total + jnp.where(active, dweight, 0.0)
        outgoing = passed_along(result, "section", -1)
        return (outgoing, total)

    zero_grad = jnp.zeros((feats, feats), jnp.float32)
    last_grad, total = lax.fori_loop(0, steps, backward_step, (start, zero_grad))
    partial_value = total[None]
    summed = lax.psum(partial_value.astype(jnp.bfloat16), "dom").astype(jnp.float32)
    nodes = rows * lax.axis_size("dom")
    return summed * (1.0 / math.sqrt(count * nodes))


def solution(mesh):
    in_specs = (
        P(None, "dom", None),
        P(None, "dom", None),
        P("section", None, None),
        P("dom", None, None, None),
        P("dom", None),
        P("dom"),
    )
    out_specs = P("section", None, None)
    return jax.shard_map(local, mesh=mesh, in_specs=in_specs, out_specs=out_specs, check_vma=False)
```

profile of v0, /device:TPU:1, one launch (start us, length us, event | category | flops | bytes accessed | tf_op | source)
XLA Modules:
  0.0 1317.6 jit_solution(14709749336149699436)
XLA Ops:
  13.2 496.3 %while.38 = (s32[]{:T(128)}, bf16[256,256]{1,0:T(8,128)(2,1)S(1)}, f32[12,256,256]{2,1,0:T(8,128)}, f32[12,256,256]{2,1,0:T(8,128)}, pred[]{:T(512)}, /*index=5*...) while((s32[]{:T(128)}, bf16[256,256]{1,0:T(8,128)(2,1)S(1)}, ...), condition=%wide.region_3.4_spmd, body=%wide.region_1.3_spmd.sunk | while | flops 136381808 | bytes 8531119 | solution.py:147
  124.0 6.2 collective-permute-start.2
  142.9 6.2 collective-permute-start.2
  161.7 6.2 collective-permute-start.2
  180.6 6.2 collective-permute-start.2
  199.5 6.2 collective-permute-start.2
  218.3 6.2 collective-permute-start.2
  237.2 6.2 collective-permute-start.2
  256.1 6.2 collective-permute-start.2
  274.9 6.2 collective-permute-start.2
  293.8 6.2 collective-permute-start.2
  312.7 6.2 collective-permute-start.2
  331.5 6.2 collective-permute-start.2
  350.4 6.2 collective-permute-start.2
  369.3 6.2 collective-permute-start.2
  388.1 6.2 collective-permute-start.2
  407.0 6.2 collective-permute-start.2
  425.9 6.2 collective-permute-start.2
  444.8 6.2 collective-permute-start.2
  463.6 6.2 collective-permute-start.2
  482.5 6.2 collective-permute-start.2
  501.4 6.2 collective-permute-start.2
  509.5 730.7 %while.39 = (s32[]{:T(128)}, bf16[256,256]{1,0:T(8,128)(2,1)S(1)}, f32[256,256]{1,0:T(8,128)S(1)}, pred[]{:T(512)}, s32[]{:T(128)}, /*index=5*/bf16[12,256,256]{...) while((s32[]{:T(128)}, bf16[256,256]{1,0:T(8,128)(2,1)S(1)}, ...), condition=%wide.region_7.8_spmd.clone, body=%wide.region_4.7_spmd.clone.sunk | while | flops 189399392 | bytes 17312208 | solution.py:164
  531.0 5.9 collective-permute-done.5
  558.4 5.9 collective-permute-done.5
  585.9 5.9 collective-permute-done.5
  613.3 5.9 collective-permute-done.5
  640.7 5.5 collective-permute-done.5
  829.7 5.5 collective-permute-done.5
  937.7 5.5 collective-permute-done.5
  1045.7 5.5 collective-permute-done.5
  1240.9 68.3 %all-reduce.2.cloned.1.call-done = bf16[1,256,256]{2,1,0:T(8,128)(2,1)} async-done(((bf16[1,256,256]{2,1,0:T(8,128)(2,1)}), bf16[1,256,256]{2,1,0:T(8,128)(2,1)}) %all-reduce.2.cloned.1.call-update) | async-done | bytes 131088 | tf_op jit(solution)/shard_map/psum | solution.py:166
  (1308 shorter events, 1052.0 us)
Async XLA Ops:
  6.5 1302.6 %all-reduce.2.cloned.1.call-start = ((), (), s32[]{:S(2)}) async-start(), calls=%async_computation | async-start | bytes 262144 | tf_op jit(solution)/shard_map/psum | solution.py:166
  63.3 8.2 collective-permute-start
  80.0 8.2 collective-permute-start
  96.8 8.2 collective-permute-start
  114.2 8.2 collective-permute-start
  133.0 8.2 collective-permute-start
  142.9 8.1 collective-permute-start.2
  151.9 8.2 collective-permute-start
  170.8 8.2 collective-permute-start
  189.7 8.2 collective-permute-start
  208.5 8.2 collective-permute-start
  218.3 8.1 collective-permute-start.2
  227.4 8.2 collective-permute-start
  246.3 8.2 collective-permute-start
  265.1 8.2 collective-permute-start
  284.0 8.2 collective-permute-start
  293.8 8.1 collective-permute-start.2
  302.9 8.2 collective-permute-start
  321.7 8.2 collective-permute-start
  340.6 8.2 collective-permute-start
  359.5 8.2 collective-permute-start
  378.3 8.2 collective-permute-start
  397.2 8.2 collective-permute-start
  416.1 8.2 collective-permute-start
  434.9 8.2 collective-permute-start
  453.8 8.2 collective-permute-start
  472.7 8.2 collective-permute-start
  491.5 8.2 collective-permute-start
  528.4 8.5 collective-permute-start.5
  555.8 8.5 collective-permute-start.5
  583.3 8.5 collective-permute-start.5
  610.7 8.5 collective-permute-start.5
  (186 other events, 1524.2 us)
Sparse Core Ops, SparseCore 0:
  1241.0 68.0 all-reduce.1
where the time goes:
time: 1330 us; the launch traced here: 1320 us
  starting transfers between devices  568 us (43%)
  waiting for transfers between devices  258 us (19%)
  other arithmetic  176 us (13%)
  matrix products  173 us (13%)
  local copies, waits for them, and re-layouts  120 us (9%)
  between operations  13.4 us (1%)
    ppermute x54, starting transfers between devices, extended(): lax.ppermute(tail, axis, [(i, (i + 1) % count) for i in range(ends)])  274 us
    ppermute x54, starting transfers between devices, passed_along(): return lax.ppermute(array, axis, pairs)  189 us
    ppermute x54, waiting for transfers between devices, passed_along(): return lax.ppermute(array, axis, pairs)  154 us
    ppermute x54, starting transfers between devices, extended(): lax.ppermute(head, axis, [((i + 1) % count, i) for i in range(ends)])  105 us
    psum x1, waiting for transfers between devices, local(): lax.psum(partial_value.astype(jnp.bfloat16), 'dom').astype(jnp.float32)  68.3 us
    dot_general x27, local copies, waits for them, and re-layouts, backward_layer(): jnp.einsum('bkij,bih->bkjh', masked, dsum, preferred_element_type=jnp.flo...  57.6 us
    dynamic_update_slice x27, other arithmetic, update(): lax.dynamic_update_index_in_dim(item, jnp.where(active, fresh, older), sl...  49.1 us
    dot_general x27, matrix products, backward_layer(): jnp.einsum('bkc,bkjh->cjh', onehot, dpicked, precision=lax.Precision.HIGH...  46 us
  transfers between devices with their start and end apart: 163, of which 109 were waited for; matrix products, arithmetic and copies ran while one was open for 9% of the time, Pallas kernels for 0%

commit v1 on v0

v1 whole, which is shorter than its diff:
```python
import functools
import math

import jax
import jax.numpy as jnp
from jax import lax
from jax.experimental import pallas as pl
from jax.experimental.pallas import tpu as pltpu
from jax.sharding import PartitionSpec as P

EPSILON = 1e-06
MESH = pl.DeviceIdType.MESH
F32 = jnp.float32
BF16 = jnp.bfloat16

BS = 128
PAIR = 2 * BS
WIN = 4 * BS
HALF = 4
ROWS = HALF * PAIR


def mm(a, b):
    return jnp.dot(a, b, preferred_element_type=F32)


def mm_tn(a, b):
    return lax.dot_general(a, b, (((0,), (0,)), ((), ())), preferred_element_type=F32)


def mm_nt(a, b):
    return lax.dot_general(a, b, (((1,), (1,)), ((), ())), preferred_element_type=F32)


def rows(p, offset=0, size=PAIR):
    return pl.ds(p * PAIR + offset, size)


def kernel(
    scaling, snaps, layers,
    src_ref, cnt_ref, tiles_ref, w_ref, feat_ref, cot_ref, out_ref,
    asend, abuf, atbuf, wbuf, hbuf, cotb, gbuf, nrmb, dsb, scb,
    gsend, grecv, dwst, dwrecv, outg,
    f_send, f_recv, w_send, w_recv, a_send, a_recv, c_send, c_recv,
    h_send, h_recv, g_send, g_recv, d_send, d_recv, o_send, o_recv,
):
    sec = lax.axis_index("section")
    dom = lax.axis_index("dom")
    x, core = dom // 2, dom % 2
    active = sec < snaps
    host_x = lax.rem(sec // 4 + lax.rem(sec, 4), 4)
    is_host = jnp.logical_and(active, x == host_x)
    half = dom // 4
    mirrored = half == 0
    place = jnp.where(mirrored, 3 - dom, dom - 4)
    target = host_x * 2 + half
    other = host_x * 2 + 1 - half
    partner = x * 2 + 1 - core
    slots = [jnp.where(mirrored, 1 - j, j) for j in range(2)]

    def push(src, dst, send, recv, to_sec, to_dom, guard):
        here = jnp.logical_and(to_sec == sec, to_dom == dom)

        @pl.when(jnp.logical_and(guard, here))
        def _():
            pltpu.make_async_copy(src, dst, recv).start()

        @pl.when(jnp.logical_and(guard, jnp.logical_not(here)))
        def _():
            pltpu.make_async_remote_copy(
                src_ref=src, dst_ref=dst, send_sem=send, recv_sem=recv,
                device_id=(to_sec, to_dom), device_id_type=MESH,
            ).start()

    def sent(src, dst, send, recv, to_sec, to_dom, guard):
        here = jnp.logical_and(to_sec == sec, to_dom == dom)

        @pl.when(jnp.logical_and(guard, jnp.logical_not(here)))
        def _():
            pltpu.make_async_remote_copy(
                src_ref=src, dst_ref=dst, send_sem=send, recv_sem=recv,
                device_id=(to_sec, to_dom), device_id_type=MESH,
            ).wait_send()

    def arrived(src, dst, recv):
        pltpu.make_async_copy(src, dst, recv).wait()

    def block(q):
        return pl.ds(pl.multiple_of(q * BS, BS), BS)

    gifts = []
    for j in range(2):
        q = 2 * place + slots[j]
        gifts.append((
            feat_ref.at[jnp.minimum(sec, snaps - 1), pl.ds(j * BS, BS)], hbuf.at[0, block(q + 1)],
            f_send.at[j], f_recv.at[q], sec, target, active,
        ))
    edge = jnp.where(mirrored, 1, 0)
    gifts.append((
        feat_ref.at[jnp.minimum(sec, snaps - 1), block(edge)], hbuf.at[0, pl.ds(0, BS)],
        f_send.at[2], f_recv.at[8], sec, other,
        jnp.logical_and(active, jnp.logical_or(dom == 3, dom == 4)),
    ))
    for gift in gifts:
        push(*gift)
    cots = []
    for j in range(2):
        q = 2 * place + slots[j]
        cots.append((
            cot_ref.at[jnp.minimum(sec, snaps - 1), pl.ds(j * BS, BS)], cotb.at[block(q)],
            c_send.at[j], c_recv.at[q], sec, target, active,
        ))

    lends = []
    for j in range(3):
        to_sec = 4 * j + lax.rem(x - j + 4, 4)
        lends.append((
            w_ref.at[0], wbuf.at[sec], w_send.at[j], w_recv.at[sec], to_sec, dom, True,
        ))
    for lend in lends:
        push(*lend)

    adj = (asend, abuf.at[place], a_send, a_recv.at[place], sec, target, active)

    @pl.when(active)
    def _():
        first = 2 * dom - 1
        for b in range(2):
            want = []
            for k in range(6):
                loc = src_ref[b, k] - first
                loc = jnp.where(mirrored, 3 - loc, loc)
                want.append(jnp.where(k < cnt_ref[b], loc, -1))
            parts = []
            for c in range(4):
                total = jnp.zeros((BS, BS), F32)
                for k in range(6):
                    keep = jnp.where(want[k] == c, 1.0, 0.0).astype(F32)
                    total = total + tiles_ref[b, k].astype(F32) * keep
                parts.append(total)
            degree = jnp.sum(parts[0] + parts[1] + parts[2] + parts[3], axis=-1, keepdims=True)
            scale = 1.0 / degree
            for c in range(4):
                asend[block(slots[b]), pl.ds(c * BS, BS)] = (parts[c] * scale).astype(BF16)

    push(*adj)
    for cot in cots:
        push(*cot)

    @pl.when(is_host)
    def _():
        for s in range(2):
            hbuf[s, pl.ds(ROWS + BS, BS)] = jnp.zeros((BS, hbuf.shape[2]), BF16)
        for q in range(9):
            dst = hbuf.at[0, pl.ds((q + 1) % 9 * BS, BS)]
            arrived(dst, dst, f_recv.at[q])
        for p in range(HALF):
            arrived(abuf.at[p], abuf.at[p], a_recv.at[p])

        def halo(slot):
            return pltpu.make_async_remote_copy(
                src_ref=hbuf.at[slot, pl.ds(BS, BS)], dst_ref=hbuf.at[slot, pl.ds(0, BS)],
                send_sem=h_send.at[slot], recv_sem=h_recv.at[slot],
                device_id=(sec, partner), device_id_type=MESH,
            )

        def forward(layer, last):
            now = lax.rem(layer, 2)
            later = 1 - now
            arrived(wbuf.at[layer], wbuf.at[layer], w_recv.at[layer])
            if last:
                halo(now).wait_recv()
            else:

                @pl.when(layer > 0)
                def _():
                    halo(now).wait_recv()

            for p in range(HALF):
                agg = mm(abuf[p], hbuf[now, pl.ds(p * PAIR, WIN)])
                scale = lax.rsqrt(jnp.mean(agg * agg, axis=-1, keepdims=True) + EPSILON)
                nrm = (agg * scale).astype(BF16)
                nrmb[layer, rows(p)] = nrm
                scb[layer, rows(p)] = jnp.broadcast_to(scale, (PAIR, 128))
                hz = 0.5 * mm(nrm, wbuf[layer])
                t = jnp.tanh(hz)
                u = 1.0 + t
                dsb[layer, rows(p)] = (0.5 * u) * (1.0 + hz * (1.0 - t))
                if not last:
                    old = hbuf[now, rows(p, BS)].astype(F32)
                    hbuf[later, rows(p, BS)] = (old + hz * u).astype(BF16)
                    if p == 0:
                        halo(later).start()
            if not last:
                halo(later).wait_send()

        def forward_step(layer, carry):
            forward(layer, False)
            return carry

        lax.fori_loop(0, layers - 1, forward_step, 0)
        forward(layers - 1, True)

        for p in range(HALF):
            atbuf[p] = abuf[p].T
        for q in range(8):
            arrived(cotb.at[pl.ds(q * BS, BS)], cotb.at[pl.ds(q * BS, BS)], c_recv.at[q])
        gbuf[...] = cotb[...].astype(F32)

        giver = sec * 2 + core

        def rim(slot):
            return pltpu.make_async_remote_copy(
                src_ref=gsend.at[slot], dst_ref=grecv.at[slot],
                send_sem=g_send.at[slot], recv_sem=g_recv.at[slot],
                device_id=(sec, partner), device_id_type=MESH,
            )

        def shares(layer, slot):
            return [
                (
                    dwst.at[slot, pl.ds(e * 32, 32)], dwrecv.at[giver],
                    d_send.at[slot, e], d_recv.at[giver], layer, e, True,
                )
                for e in range(8)
            ]

        def backward(layer, last):
            slot = lax.rem(layer, 2)
            total = None
            daggs = []
            for p in range(HALF):
                dz = (gbuf[rows(p)] * dsb[layer, rows(p)]).astype(BF16)
                nrm = nrmb[layer, rows(p)]
                if not last:
                    dnrm = mm_nt(dz, wbuf[layer])
                    wide = nrm.astype(F32)
                    mean = jnp.mean(dnrm * wide, axis=-1, keepdims=True)
                    scale = scb[layer, rows(p)][:, :1]
                    dagg = (scale * (dnrm - wide * mean)).astype(BF16)
                    daggs.append(dagg)
                    if p == 0:
                        gsend[slot] = mm(atbuf[0, pl.ds(0, BS)], dagg).astype(BF16)
                        rim(slot).start()
                term = mm_tn(nrm, dz)
                total = term if total is None else total + term
            if not last:
                spread = [mm(atbuf[0, pl.ds(BS, WIN - BS)], daggs[0])]
                spread += [mm(atbuf[p], daggs[p]) for p in range(1, HALF)]
                for p in range(HALF):
                    lo = 0 if p == 0 else BS
                    low = spread[p][lo : lo + BS]
                    high = spread[p][lo + BS : lo + PAIR]
                    if p > 0:
                        tail = 2 * BS if p == 1 else 3 * BS
                        low = low + spread[p - 1][tail : tail + BS]
                    if p < HALF - 1:
                        high = high + spread[p + 1][:BS]
                    gbuf[rows(p, 0, BS)] = gbuf[rows(p, 0, BS)] + low
                    gbuf[rows(p, BS, BS)] = gbuf[rows(p, BS, BS)] + high

            def drain():
                for share in shares(layer + 2, slot):
                    sent(*share)

            if last:
                drain()
            else:
                pl.when(layer < layers - 2)(drain)
            dwst[slot] = total.astype(BF16)
            for share in shares(layer, slot):
                push(*share)

            @pl.when(layer == sec)
            def _():
                own = dwst.at[slot, pl.ds(pl.multiple_of(dom * 32, 32), 32)]
                arrived(own, dwrecv.at[giver], d_recv.at[giver])

            if not last:
                rim(slot).wait()
                gbuf[pl.ds(0, BS)] = gbuf[pl.ds(0, BS)] + grecv[slot].astype(F32)

        def backward_step(step, carry):
            backward(layers - 1 - step, False)
            return carry

        lax.fori_loop(0, layers - 1, backward_step, 0)
        backward(0, True)
        for layer in (1, 0):
            for share in shares(layer, layer % 2):
                sent(*share)

    for gift in gifts + lends + [adj] + cots:
        sent(*gift)

    total = jnp.zeros((32, dwrecv.shape[2]), F32)
    for g in range(2 * snaps):

        @pl.when(jnp.logical_not(jnp.logical_and(is_host, sec * 2 + core == g)))
        def _():
            arrived(dwrecv.at[g], dwrecv.at[g], d_recv.at[g])

        total = total + dwrecv[g].astype(F32)
    outg[dom] = total * scaling

    def gathered(k):
        return pltpu.make_async_remote_copy(
            src_ref=outg.at[dom], dst_ref=outg.at[dom],
            send_sem=o_send.at[k], recv_sem=o_recv.at[dom],
            device_id=(sec, lax.rem(dom + k + 1, 8)), device_id_type=MESH,
        )

    for k in range(7):
        gathered(k).start()
    for k in range(7):
        e = lax.rem(dom + k + 1, 8)
        arrived(outg.at[e], outg.at[e], o_recv.at[e])
    for k in range(7):
        gathered(k).wait_send()
    for e in range(8):
        out_ref[0, pl.ds(e * 32, 32)] = outg[e]


def local(features, cotangent, weights, tiles, sources, counts):
    snaps, nodes, feats = features.shape
    layers = lax.axis_size("section")
    doms = lax.axis_size("dom")
    assert (layers, doms, snaps, nodes, feats) == (16, 8, 12, 256, 256)
    scaling = 1.0 / math.sqrt(snaps * nodes * doms)
    vmem = pl.BlockSpec(memory_space=pltpu.VMEM)
    smem = pl.BlockSpec(memory_space=pltpu.SMEM)
    hbm = pl.BlockSpec(memory_space=pl.ANY)
    dma = pltpu.SemaphoreType.DMA
    return pl.pallas_call(
        functools.partial(kernel, scaling, snaps, layers),
        out_shape=jax.ShapeDtypeStruct((1, feats, feats), F32),
        in_specs=[smem, smem, vmem, vmem, hbm, hbm],
        out_specs=vmem,
        scratch_shapes=[
            pltpu.VMEM((PAIR, WIN), BF16),
            pltpu.VMEM((HALF, PAIR, WIN), BF16),
            pltpu.VMEM((HALF, WIN, PAIR), BF16),
            pltpu.VMEM((layers, feats, feats), BF16),
            pltpu.VMEM((2, ROWS + 2 * BS, feats), BF16),
            pltpu.VMEM((ROWS, feats), BF16),
            pltpu.VMEM((ROWS, feats), F32),
            pltpu.VMEM((layers, ROWS, feats), BF16),
            pltpu.VMEM((layers, ROWS, feats), F32),
            pltpu.VMEM((layers, ROWS, 128), F32),
            pltpu.VMEM((2, BS, feats), BF16),
            pltpu.VMEM((2, BS, feats), BF16),
            pltpu.VMEM((2, feats, feats), BF16),
            pltpu.VMEM((2 * snaps, 32, feats), BF16),
            pltpu.VMEM((8, 32, feats), F32),
            dma((3,)), dma((9,)), dma((3,)), dma((layers,)),
            dma, dma((HALF,)), dma((2,)), dma((8,)),
            dma((2,)), dma((2,)), dma((2,)), dma((2,)),
            dma((2, 8)), dma((2 * snaps,)), dma((7,)), dma((8,)),
        ],
        compiler_params=pltpu.CompilerParams(
            has_side_effects=True, vmem_limit_bytes=60 * 1024 * 1024
        ),
    )(sources, counts, tiles, weights, features, cotangent)


def solution(mesh):
    in_specs = (
        P(None, "dom", None),
        P(None, "dom", None),
        P("section", None, None),
        P("dom", None, None, None),
        P("dom", None),
        P("dom"),
    )
    out_specs = P("section", None, None)
    return jax.shard_map(local, mesh=mesh, in_specs=in_specs, out_specs=out_specs, check_vma=False)
```

time: 1330 us -> 114 us (0.09)
  starting transfers between devices: 568 us -> 0 us
  waiting for transfers between devices: 258 us -> 0 us
  other arithmetic: 176 us -> 0 us
  matrix products: 173 us -> 0 us
  local copies, waits for them, and re-layouts: 120 us -> 1.67 us
  Pallas kernels: 0 us -> 112 us
  between operations: 13.4 us -> 0.01 us
    ppermute x162 -> x0, starting transfers between devices: 568 us -> none  [the longest x54 274 us: extended(): lax.ppermute(tail, axis, [(i, (i + 1) % count) for i in range(ends)])]
    ppermute x162 -> x0, waiting for transfers between devices: 190 us -> none  [the longest x54 154 us: passed_along(): return lax.ppermute(array, axis, pairs)]
    dot_general x162 -> x0, matrix products: 173 us -> none  [the longest x27 46 us: backward_layer(): jnp.einsum('bkc,bkjh->cjh', onehot, dpicked, precision=lax.Precision.HIGH...]
    pallas_call x0 -> x1, Pallas kernels: none -> 112 us  [local(): pl.pallas_call(functools.partial(kernel, scaling, snaps, layers), out_sha...]
    psum x1 -> x0, waiting for transfers between devices: 68.3 us -> none  [local(): lax.psum(partial_value.astype(jnp.bfloat16), 'dom').astype(jnp.float32)]
    convert_element_type x83 -> x0, other arithmetic: 61.4 us -> none  [the longest x27 30.9 us: backward_layer(): dz_val = (grad * sig * (1.0 + z_val * (1.0 - sig))).astype(jnp.bfloat16)]
    dot_general x27 -> x0, local copies, waits for them, and re-layouts: 57.6 us -> none  [backward_layer(): jnp.einsum('bkij,bih->bkjh', masked, dsum, preferred_element_type=jnp.flo...]
    dynamic_update_slice x27 -> x0, other arithmetic: 49.1 us -> none  [update(): lax.dynamic_update_index_in_dim(item, jnp.where(active, fresh, older), sl...]
  transfers between devices with their start and end apart: 163 -> 0, of which waited for: 109 -> 0; matrix products, arithmetic and copies ran while one was open for 9% -> 0% of each run, Pallas kernels for 0% -> 0%
where the time goes in v1:
time: 114 us
  Pallas kernels  112 us (98%)
  local copies, waits for them, and re-layouts  1.67 us (1%)
    pallas_call x1, Pallas kernels, local(): pl.pallas_call(functools.partial(kernel, scaling, snaps, layers), out_sha...  112 us

profile of v1, /device:TPU:1, one launch (start us, length us, event | category | flops | bytes accessed | tf_op | source)
XLA Modules:
  0.0 114.2 jit_solution(15712478925449018274)
XLA Ops:
  0.0 112.5 %shard_map.64 = f32[1,256,256]{2,1,0:T(8,128)} custom-call(s32[2,6]{1,0:T(2,128)} %src_ref.1, s32[2]{0:T(128)} %cnt_ref.1, bf16[2,6,128,128]{3,2,1,0:T(8,128)(2,1)} %tiles_ref.1, bf16[1,256,256]{2,1,0:T(8,128)(2,1)} %w_ref.1, bf16[12,256,256]{2,1,0:T(8,128)(2,1)} %feat_ref.1, bf16[12,256,256]{2,1,0:T(8,128)(2,1)} %cot_ref.1), custom_call_target="tpu_custom_call" | custom-call | tf_op jit(solution)/shard_map/pallas_call | solution.py:334
  112.5 1.7 %copy.8 = f32[1,256,256]{2,1,0:T(8,128)} copy(f32[1,256,256]{2,1,0:T(8,128)} %shard_map.64) | data formatting | bytes 524288

commit v2 on v1

--- a/solution.py
+++ b/solution.py
@@ -18,6 +18,7 @@
 WIN = 4 * BS
 HALF = 4
 ROWS = HALF * PAIR
+AHEAD = 4
 
 
 def mm(a, b):
@@ -40,9 +41,10 @@
     scaling, snaps, layers,
     src_ref, cnt_ref, tiles_ref, w_ref, feat_ref, cot_ref, out_ref,
     asend, abuf, atbuf, wbuf, hbuf, cotb, gbuf, nrmb, dsb, scb,
-    gsend, grecv, dwst, dwrecv, outg,
+    gsend, grecv, keep, lent, fetched, dwst, dwrecv, outg,
     f_send, f_recv, w_send, w_recv, a_send, a_recv, c_send, c_recv,
-    h_send, h_recv, g_send, g_recv, d_send, d_recv, o_send, o_recv,
+    v_send, v_recv, h_send, h_recv, g_send, g_recv, p_send, p_recv,
+    d_send, d_recv, o_send, o_recv,
 ):
     sec = lax.axis_index("section")
     dom = lax.axis_index("dom")
@@ -58,6 +60,19 @@
     partner = x * 2 + 1 - core
     slots = [jnp.where(mirrored, 1 - j, j) for j in range(2)]
 
+    barrier = pltpu.get_barrier_semaphore()
+    for k in range(1, 8):
+        pl.semaphore_signal(
+            barrier, inc=1, device_id=(sec, lax.rem(dom + k, 8)), device_id_type=MESH
+        )
+
+    @pl.when(is_host)
+    def _():
+        for k in range(1, 16):
+            pl.semaphore_signal(
+                barrier, inc=1, device_id=(lax.rem(sec + k, 16), dom), device_id_type=MESH
+            )
+
     def push(src, dst, send, recv, to_sec, to_dom, guard):
         here = jnp.logical_and(to_sec == sec, to_dom == dom)
 
@@ -87,40 +102,6 @@
 
     def block(q):
         return pl.ds(pl.multiple_of(q * BS, BS), BS)
-
-    gifts = []
-    for j in range(2):
-        q = 2 * place + slots[j]
-        gifts.append((
-            feat_ref.at[jnp.minimum(sec, snaps - 1), pl.ds(j * BS, BS)], hbuf.at[0, block(q + 1)],
-            f_send.at[j], f_recv.at[q], sec, target, active,
-        ))
-    edge = jnp.where(mirrored, 1, 0)
-    gifts.append((
-        feat_ref.at[jnp.minimum(sec, snaps - 1), block(edge)], hbuf.at[0, pl.ds(0, BS)],
-        f_send.at[2], f_recv.at[8], sec, other,
-        jnp.logical_and(active, jnp.logical_or(dom == 3, dom == 4)),
-    ))
-    for gift in gifts:
-        push(*gift)
-    cots = []
-    for j in range(2):
-        q = 2 * place + slots[j]
-        cots.append((
-            cot_ref.at[jnp.minimum(sec, snaps - 1), pl.ds(j * BS, BS)], cotb.at[block(q)],
-            c_send.at[j], c_recv.at[q], sec, target, active,
-        ))
-
-    lends = []
-    for j in range(3):
-        to_sec = 4 * j + lax.rem(x - j + 4, 4)
-        lends.append((
-            w_ref.at[0], wbuf.at[sec], w_send.at[j], w_recv.at[sec], to_sec, dom, True,
-        ))
-    for lend in lends:
-        push(*lend)
-
-    adj = (asend, abuf.at[place], a_send, a_recv.at[place], sec, target, active)
 
     @pl.when(active)
     def _():
@@ -143,7 +124,42 @@
             for c in range(4):
                 asend[block(slots[b]), pl.ds(c * BS, BS)] = (parts[c] * scale).astype(BF16)
 
+    pl.semaphore_wait(barrier, jnp.where(is_host, 9, 10))
+
+    gifts = []
+    for j in range(2):
+        q = 2 * place + slots[j]
+        gifts.append((
+            feat_ref.at[jnp.minimum(sec, snaps - 1), pl.ds(j * BS, BS)], hbuf.at[0, block(q + 1)],
+            f_send.at[j], f_recv.at[q], sec, target, active,
+        ))
+    edge = jnp.where(mirrored, 1, 0)
+    gifts.append((
+        feat_ref.at[jnp.minimum(sec, snaps - 1), block(edge)], hbuf.at[0, pl.ds(0, BS)],
+        f_send.at[2], f_recv.at[8], sec, other,
+        jnp.logical_and(active, jnp.logical_or(dom == 3, dom == 4)),
+    ))
+    for gift in gifts:
+        push(*gift)
+    adj = (asend, abuf.at[place], a_send, a_recv.at[place], sec, target, active)
     push(*adj)
+    cots = []
+    for j in range(2):
+        q = 2 * place + slots[j]
+        cots.append((
+            cot_ref.at[jnp.minimum(sec, snaps - 1), pl.ds(j * BS, BS)], cotb.at[block(q)],
+            c_send.at[j], c_recv.at[q], sec, target, active,
+        ))
+
+    mine = block(core)
+    lends = []
+    for j in range(3):
+        to_sec = 4 * j + lax.rem(x - j + 4, 4)
+        lends.append((
+            w_ref.at[0, mine], wbuf.at[sec, mine], w_send.at[j], w_recv.at[sec], to_sec, dom, True,
+        ))
+    for lend in lends:
+        push(*lend)
     for cot in cots:
         push(*cot)
 
@@ -151,6 +167,19 @@
     def _():
         for s in range(2):
             hbuf[s, pl.ds(ROWS + BS, BS)] = jnp.zeros((BS, hbuf.shape[2]), BF16)
+        def swap(layer):
+            return pltpu.make_async_remote_copy(
+                src_ref=wbuf.at[layer, mine], dst_ref=wbuf.at[layer, mine],
+                send_sem=v_send.at[layer], recv_sem=v_recv.at[layer],
+                device_id=(sec, partner), device_id_type=MESH,
+            )
+
+        def relay(layer):
+            arrived(wbuf.at[layer, mine], wbuf.at[layer, mine], w_recv.at[layer])
+            swap(layer).start()
+
+        for layer in range(AHEAD):
+            relay(layer)
         for q in range(9):
             dst = hbuf.at[0, pl.ds((q + 1) % 9 * BS, BS)]
             arrived(dst, dst, f_recv.at[q])
@@ -167,7 +196,14 @@
         def forward(layer, last):
             now = lax.rem(layer, 2)
             later = 1 - now
-            arrived(wbuf.at[layer], wbuf.at[layer], w_recv.at[layer])
+            if not last:
+
+                @pl.when(layer < layers - AHEAD)
+                def _():
+                    relay(layer + AHEAD)
+
+            theirs = block(1 - core)
+            arrived(wbuf.at[layer, theirs], wbuf.at[layer, theirs], v_recv.at[layer])
             if last:
                 halo(now).wait_recv()
             else:
@@ -207,8 +243,6 @@
             arrived(cotb.at[pl.ds(q * BS, BS)], cotb.at[pl.ds(q * BS, BS)], c_recv.at[q])
         gbuf[...] = cotb[...].astype(F32)
 
-        giver = sec * 2 + core
-
         def rim(slot):
             return pltpu.make_async_remote_copy(
                 src_ref=gsend.at[slot], dst_ref=grecv.at[slot],
@@ -216,14 +250,28 @@
                 device_id=(sec, partner), device_id_type=MESH,
             )
 
-        def shares(layer, slot):
+        def joint(layer):
+            return pltpu.make_async_remote_copy(
+                src_ref=lent.at[layer], dst_ref=fetched.at[layer],
+                send_sem=p_send.at[layer], recv_sem=p_recv.at[layer],
+                device_id=(sec, partner), device_id_type=MESH,
+            )
+
+        def shares(layer):
             return [
                 (
-                    dwst.at[slot, pl.ds(e * 32, 32)], dwrecv.at[giver],
-                    d_send.at[slot, e], d_recv.at[giver], layer, e, True,
+                    dwst.at[layer, pl.ds(e * 32, 32)], dwrecv.at[sec],
+                    d_send.at[layer, e], d_recv.at[sec], layer, core * 4 + e, True,
                 )
-                for e in range(8)
+                for e in range(4)
             ]
+
+        def deliver(layer):
+            joint(layer).wait_recv()
+            both = keep[lax.rem(layer, 2)] + fetched[layer].astype(F32)
+            dwst[layer] = both.astype(BF16)
+            for share in shares(layer):
+                push(*share)
 
         def backward(layer, last):
             slot = lax.rem(layer, 2)
@@ -259,22 +307,18 @@
                     gbuf[rows(p, 0, BS)] = gbuf[rows(p, 0, BS)] + low
                     gbuf[rows(p, BS, BS)] = gbuf[rows(p, BS, BS)] + high
 
-            def drain():
-                for share in shares(layer + 2, slot):
-                    sent(*share)
-
+            total = jnp.where(core == 0, total, jnp.concatenate([total[BS:], total[:BS]], axis=0))
+            keep[slot] = total[:BS]
+            lent[layer] = total[BS:].astype(BF16)
+            joint(layer).start()
             if last:
-                drain()
+                deliver(1)
+                deliver(0)
             else:
-                pl.when(layer < layers - 2)(drain)
-            dwst[slot] = total.astype(BF16)
-            for share in shares(layer, slot):
-                push(*share)
-
-            @pl.when(layer == sec)
-            def _():
-                own = dwst.at[slot, pl.ds(pl.multiple_of(dom * 32, 32), 32)]
-                arrived(own, dwrecv.at[giver], d_recv.at[giver])
+
+                @pl.when(layer < layers - 1)
+                def _():
+                    deliver(layer + 1)
 
             if not last:
                 rim(slot).wait()
@@ -286,22 +330,24 @@
 
         lax.fori_loop(0, layers - 1, backward_step, 0)
         backward(0, True)
-        for layer in (1, 0):
-            for share in shares(layer, layer % 2):
+
+        def settle(layer, carry):
+            swap(layer).wait_send()
+            joint(layer).wait_send()
+            for share in shares(layer):
                 sent(*share)
+            return carry
+
+        lax.fori_loop(0, layers, settle, 0)
 
     for gift in gifts + lends + [adj] + cots:
         sent(*gift)
 
     total = jnp.zeros((32, dwrecv.shape[2]), F32)
-    for g in range(2 * snaps):
-
-        @pl.when(jnp.logical_not(jnp.logical_and(is_host, sec * 2 + core == g)))
-        def _():
-            arrived(dwrecv.at[g], dwrecv.at[g], d_recv.at[g])
-
+    for g in range(snaps):
+        arrived(dwrecv.at[g], dwrecv.at[g], d_recv.at[g])
         total = total + dwrecv[g].astype(F32)
-    outg[dom] = total * scaling
+    outg[dom] = (total * scaling).astype(BF16)
 
     def gathered(k):
         return pltpu.make_async_remote_copy(
@@ -318,7 +364,7 @@
     for k in range(7):
         gathered(k).wait_send()
     for e in range(8):
-        out_ref[0, pl.ds(e * 32, 32)] = outg[e]
+        out_ref[0, pl.ds(e * 32, 32)] = outg[e].astype(F32)
 
 
 def local(features, cotangent, weights, tiles, sources, counts):
@@ -349,16 +395,20 @@
             pltpu.VMEM((layers, ROWS, 128), F32),
             pltpu.VMEM((2, BS, feats), BF16),
             pltpu.VMEM((2, BS, feats), BF16),
-            pltpu.VMEM((2, feats, feats), BF16),
-            pltpu.VMEM((2 * snaps, 32, feats), BF16),
-            pltpu.VMEM((8, 32, feats), F32),
+            pltpu.VMEM((2, BS, feats), F32),
+            pltpu.VMEM((layers, BS, feats), BF16),
+            pltpu.VMEM((layers, BS, feats), BF16),
+            pltpu.VMEM((layers, BS, feats), BF16),
+            pltpu.VMEM((snaps, 32, feats), BF16),
+            pltpu.VMEM((8, 32, feats), BF16),
             dma((3,)), dma((9,)), dma((3,)), dma((layers,)),
             dma, dma((HALF,)), dma((2,)), dma((8,)),
-            dma((2,)), dma((2,)), dma((2,)), dma((2,)),
-            dma((2, 8)), dma((2 * snaps,)), dma((7,)), dma((8,)),
+            dma((layers,)), dma((layers,)),
+            dma((2,)), dma((2,)), dma((2,)), dma((2,)), dma((layers,)), dma((layers,)),
+            dma((layers, 4)), dma((snaps,)), dma((7,)), dma((8,)),
         ],
         compiler_params=pltpu.CompilerParams(
-            has_side_effects=True, vmem_limit_bytes=60 * 1024 * 1024
+            collective_id=0, has_side_effects=True, vmem_limit_bytes=60 * 1024 * 1024
         ),
     )(sources, counts, tiles, weights, features, cotangent)
 

time: 114 us -> 104 us (0.912)
  Pallas kernels: 112 us -> 102 us
    pallas_call x1, Pallas kernels: 112 us -> 102 us  [local(): pl.pallas_call(functools.partial(kernel, scaling, snaps, layers), out_sha...]
where the time goes in v2:
time: 104 us
  Pallas kernels  102 us (98%)
  local copies, waits for them, and re-layouts  1.67 us (2%)
    pallas_call x1, Pallas kernels, local(): pl.pallas_call(functools.partial(kernel, scaling, snaps, layers), out_sha...  102 us

profile of v2, /device:TPU:1, one launch (start us, length us, event | category | flops | bytes accessed | tf_op | source)
XLA Modules:
  0.0 103.7 jit_solution(8238170459411969802)
XLA Ops:
  0.0 102.0 %shard_map.64 = f32[1,256,256]{2,1,0:T(8,128)} custom-call(s32[2,6]{1,0:T(2,128)} %src_ref.1, s32[2]{0:T(128)} %cnt_ref.1, bf16[2,6,128,128]{3,2,1,0:T(8,128)(2,1)} %tiles_ref.1, bf16[1,256,256]{2,1,0:T(8,128)(2,1)} %w_ref.1, bf16[12,256,256]{2,1,0:T(8,128)(2,1)} %feat_ref.1, bf16[12,256,256]{2,1,0:T(8,128)(2,1)} %cot_ref.1), custom_call_target="tpu_custom_call" | custom-call | tf_op jit(solution)/shard_map/pallas_call | solution.py:380
  102.0 1.7 %copy.8 = f32[1,256,256]{2,1,0:T(8,128)} copy(f32[1,256,256]{2,1,0:T(8,128)} %shard_map.64) | data formatting | bytes 524288
